TPU v7x, 256 devices: a whole 4x4x8 slice. The times are simulated.
256 devices in a mesh: dp: 32 (over y_lo, z, core), seq: 8 (over y_hi, x).
Axes of the slice: x: 4, y: 4 (y_hi: 2, y_lo: 2; y = y_hi * 2 + y_lo), z: 8, core: 2. Of those that a mesh axis runs over, the one named last changes fastest.
Arguments:
- acts: bfloat16 [32768, 4096], P(('dp', 'seq')), may hold values from -24 to 24
- grad_out: bfloat16 [32768, 4096], P('dp', 'seq'), may hold values from -6 to 6
- proj_weight: bfloat16 [4096, 4096], P('dp', 'seq'), may hold values from -0.09375 to 0.09375
Outputs:
- grad_acts: float32 [32768, 4096], P(('dp', 'seq'))
- grad_weight: float32 [4096, 4096], P('dp', 'seq')
All inputs are finite; a program needn't handle non-finite values.
Results may differ from a plain program's by a relative error of at most 0.014.
Values may be sent and summed in bfloat16 or wider, within the bound.
No kernel may reach another device: no remote copies, remote signals or barrier semaphores. Data moves between devices by JAX's collectives and lax.ppermute only.
A program may use at most 64 MiB of HBM per device.

v0:
```python
import jax
import jax.numpy as jnp
from jax import lax
from jax.sharding import PartitionSpec as P


def rounded(value):
    return lax.optimization_barrier(value.astype(jnp.bfloat16)).astype(jnp.float32)


def per_device(acts, grad_out, proj_weight):
    tok_rows = acts.shape[0]
    total_tokens = tok_rows * lax.axis_size("seq") * lax.axis_size("dp")
    full_weight = lax.all_gather(proj_weight, "dp", axis=0, tiled=True)
    whole_term = lax.dot_general(
        grad_out, full_weight, (((1,), (1,)), ((), ())), preferred_element_type=jnp.float32
    )
    summed = lax.psum_scatter(
        whole_term.astype(jnp.bfloat16), "seq", scatter_dimension=0, tiled=True
    ).astype(jnp.float32)
    gathered = lax.all_gather(acts, "seq", axis=0, tiled=True)
    local_term = None
    local_term = rounded(
        lax.dot_general(
            gathered, grad_out, (((0,), (0,)), ((), ())), preferred_element_type=jnp.float32
        )
    )
    wsummed = lax.psum_scatter(local_term, "dp", scatter_dimension=0, tiled=True)
    grad_weight = wsummed / jnp.sqrt(jnp.float32(total_tokens))
    return (summed, grad_weight)


def solution(mesh):
    in_specs = (P(("dp", "seq"), None), P("dp", "seq"), P("dp", "seq"))
    out_specs = (P(("dp", "seq"), None), P("dp", "seq"))
    return jax.shard_map(
        per_device, mesh=mesh, in_specs=in_specs, out_specs=out_specs, check_vma=False
    )
```

profile of v0, /device:TPU:4, one launch (start us, length us, event | category | flops | bytes accessed | tf_op | source)
XLA Modules:
  0.0 455.5 jit_solution(2296822489435364021)
XLA Ops:
  7.2 0.0 copy-start
  7.2 0.0 all-gather.3.cloned.1.call-start
  7.2 0.7 all-gather.3.cloned.1.call-update
  7.9 0.0 all-gather.5.cloned.1.call-start
  8.0 0.7 all-gather.5.cloned.1.call-update
  8.7 0.0 reduce-scatter.3.cloned.1.call-start
  8.7 71.0 %all-gather.3.cloned.1.call-done = bf16[4096,512]{1,0:T(8,128)(2,1)} async-done(((bf16[128,512]{1,0:T(8,128)(2,1)}), bf16[4096,512]{1,0:T(8,128)(2,1)}) %all-gather.3.cloned.1.call-update) | async-done | bytes 4194320 | tf_op jit(solution)/shard_map/all_gather | solution.py:14
  79.7 0.0 copy-done
  79.7 8.9 %convolution_convert_fusion = bf16[1024,4096]{1,0:T(8,128)(2,1)} fusion(bf16[1024,512]{1,0:T(8,128)(2,1)S(1)} %copy-done, bf16[4096,512]{1,0:T(8,128)(2,1)} %all-gather.3.cloned.1.call-done), kind=kOutput, calls=%fused_computation | convolution fusion | flops 4299161600 | bytes 13631488 | tf_op jit(solution)/shard_map/dot_general | solution.py:15
  88.6 0.0 reduce-scatter.3.cloned.1.call-update
  88.6 0.0 reduce-scatter.5.cloned.1.call-start
  88.7 105.8 %all-gather.5.cloned.1.call-done = bf16[1024,4096]{1,0:T(8,128)(2,1)} async-done(((bf16[128,4096]{1,0:T(8,128)(2,1)}), bf16[1024,4096]{1,0:T(8,128)(2,1)}) %all-gather.5.cloned.1.call-update) | async-done | bytes 8388624 | tf_op jit(solution)/shard_map/all_gather | solution.py:21
  194.5 8.4 %convolution_convert_fusion.1 = bf16[4096,512]{1,0:T(8,128)(2,1)S(1)} fusion(bf16[1024,4096]{1,0:T(8,128)(2,1)} %all-gather.5.cloned.1.call-done, bf16[1024,512]{1,0:T(8,128)(2,1)S(1)} %copy-done), kind=kOutput, calls=%fused_computation.1 | convolution fusion | flops 4297064448 | bytes 13631488 | tf_op jit(solution)/shard_map/dot_general | solution.py:24
  202.9 4.4 convert_element_type.15
  207.3 0.0 reduce-scatter.5.cloned.1.call-update
  207.3 108.8 %reduce-scatter.3.cloned.1.call-done = bf16[128,4096]{1,0:T(8,128)(2,1)} async-done(((bf16[1024,4096]{1,0:T(8,128)(2,1)}), bf16[128,4096]{1,0:T(8,128)(2,1)}) %reduce-scatter.3.cloned.1.call-update) | async-done | bytes 1048592 | tf_op jit(solution)/shard_map/reduce_scatter | solution.py:18
  316.1 2.8 convert_element_type.13
  318.9 128.4 %reduce-scatter.5.cloned.1.call-done = f32[128,512]{1,0:T(8,128)} async-done(((f32[4096,512]{1,0:T(8,128)}), f32[128,512]{1,0:T(8,128)}) %reduce-scatter.5.cloned.1.call-update) | async-done | bytes 262160 | tf_op jit(solution)/shard_map/reduce_scatter | solution.py:28
  447.2 1.7 broadcast_multiply_fusion
Async XLA Ops:
  7.2 72.5 %copy-start = (bf16[1024,512]{1,0:T(8,128)(2,1)S(1)}, bf16[1024,512]{1,0:T(8,128)(2,1)}, u32[]{:S(2)}) copy-start(bf16[1024,512]{1,0:T(8,128)(2,1)} %param.4) | copy-start | bytes 3145732
  7.2 72.5 %all-gather.3.cloned.1.call-start = ((), (), s32[]{:S(2)}) async-start(), calls=%async_computation.2 | async-start | bytes 4325376 | tf_op jit(solution)/shard_map/all_gather | solution.py:14
  7.9 186.6 %all-gather.5.cloned.1.call-start = ((), (), s32[]{:S(2)}) async-start(), calls=%async_computation.4 | async-start | bytes 9437184 | tf_op jit(solution)/shard_map/all_gather | solution.py:21
  8.7 307.4 %reduce-scatter.3.cloned.1.call-start = ((), (), s32[]{:S(2)}) async-start(), calls=%async_computation.3 | async-start | bytes 9437184 | tf_op jit(solution)/shard_map/reduce_scatter | solution.py:18
  88.6 358.6 %reduce-scatter.5.cloned.1.call-start = ((), (), s32[]{:S(2)}) async-start(), calls=%async_computation.5 | async-start | bytes 8650752 | tf_op jit(solution)/shard_map/reduce_scatter | solution.py:28
Sparse Core Ops, SparseCore 0:
  9.9 69.7 all-gather.2
  82.3 112.1 all-gather.4
  198.7 117.4 reduce-scatter.2
  318.5 128.6 reduce-scatter.4
where the time goes:
time: 456 us; the launch traced here: 455 us
  waiting for transfers between devices  415 us (91%)
  matrix products  17.3 us (4%)
  between operations  13.8 us (3%)
  other arithmetic  8.86 us (2%)
    reduce_scatter x1, waiting for transfers between devices, per_device(): lax.psum_scatter(local_term, 'dp', scatter_dimension=0, tiled=True)  128 us
    reduce_scatter x1, waiting for transfers between devices, per_device(): lax.psum_scatter(whole_term.astype(jnp.bfloat16), 'seq', scatter_dimensio...  109 us
    all_gather x1, waiting for transfers between devices, per_device(): gathered = lax.all_gather(acts, 'seq', axis=0, tiled=True)  106 us
    all_gather x1, waiting for transfers between devices, per_device(): full_weight = lax.all_gather(proj_weight, 'dp', axis=0, tiled=True)  71 us
  transfers between devices with their start and end apart: 4, of which 4 were waited for; matrix products, arithmetic and copies ran while one was open for 5% of the time, Pallas kernels for 0%

commit v1 on v0

--- a/solution.py
+++ b/solution.py
@@ -11,7 +11,9 @@
 def per_device(acts, grad_out, proj_weight):
     tok_rows = acts.shape[0]
     total_tokens = tok_rows * lax.axis_size("seq") * lax.axis_size("dp")
-    full_weight = lax.all_gather(proj_weight, "dp", axis=0, tiled=True)
+    full_weight = jnp.concatenate(
+        lax.all_to_all(jnp.stack([proj_weight] * lax.axis_size("dp")), "dp", 0, 0), axis=0
+    )
     whole_term = lax.dot_general(
         grad_out, full_weight, (((1,), (1,)), ((), ())), preferred_element_type=jnp.float32
     )

time: 456 us -> 415 us (0.910)
  waiting for transfers between devices: 415 us -> 270 us
  blocking collectives: 0 us -> 105 us
    all_to_all x0 -> x1, blocking collectives: none -> 105 us  [per_device(): lax.all_to_all(jnp.stack([proj_weight] * lax.axis_size('dp')), 'dp', 0, 0)]
    all_gather x1, waiting for transfers between devices: 106 us -> 32.8 us  [per_device(): gathered = lax.all_gather(acts, 'seq', axis=0, tiled=True)]
    all_gather x1 -> x0, waiting for transfers between devices: 71 us -> none  [per_device(): full_weight = lax.all_gather(proj_weight, 'dp', axis=0, tiled=True)]
  transfers between devices with their start and end apart: 4 -> 3, of which waited for: 4 -> 3; matrix products, arithmetic and copies ran while one was open for 5% -> 6% of each run, Pallas kernels for 0% -> 0%
where the time goes in v1:
time: 415 us
  waiting for transfers between devices  270 us (65%)
  blocking collectives  105 us (25%)
  matrix products  15.3 us (4%)
  between operations  13.8 us (3%)
  other arithmetic  8.85 us (2%)
    reduce_scatter x1, waiting for transfers between devices, per_device(): lax.psum_scatter(local_term, 'dp', scatter_dimension=0, tiled=True)  128 us
    reduce_scatter x1, waiting for transfers between devices, per_device(): lax.psum_scatter(whole_term.astype(jnp.bfloat16), 'seq', scatter_dimensio...  108 us
    all_to_all x1, blocking collectives, per_device(): lax.all_to_all(jnp.stack([proj_weight] * lax.axis_size('dp')), 'dp', 0, 0)  105 us
    all_gather x1, waiting for transfers between devices, per_device(): gathered = lax.all_gather(acts, 'seq', axis=0, tiled=True)  32.8 us
    dot_general x1, matrix products, per_device(): lax.dot_general(gathered, grad_out, (((0,), (0,)), ((), ())), preferred_e...  8.39 us
  transfers between devices with their start and end apart: 3, of which 3 were waited for; matrix products, arithmetic and copies ran while one was open for 6% of the time, Pallas kernels for 0%

profile of v1, /device:TPU:4, one launch (start us, length us, event | category | flops | bytes accessed | tf_op | source)
XLA Modules:
  0.0 414.8 jit_solution(2437311945983363870)
XLA Ops:
  7.2 0.0 copy-start
  7.2 0.0 all-gather.2.cloned.1.call-start
  7.2 0.7 all-gather.2.cloned.1.call-update
  7.9 0.0 reduce-scatter.3.cloned.1.call-start
  8.0 1.4 stack.2
  9.3 105.5 %all_to_all.5 = bf16[32,128,512]{2,1,0:T(8,128)(2,1)S(1)} all-to-all(bf16[32,128,512]{2,1,0:T(8,128)(2,1)S(1)} %stack.2), channel_id=1, replica_groups=mesh['dp'=32,'seq'=8] {'dp'}, dimensions={0} | all-to-all | bytes 8388608 | tf_op jit(solution)/shard_map/all_to_all | solution.py:15
  114.8 0.0 copy-done
  114.8 6.9 %convolution_convert_fusion = bf16[1024,4096]{1,0:T(8,128)(2,1)} fusion(bf16[1024,512]{1,0:T(8,128)(2,1)S(1)} %copy-done, bf16[4096,512]{1,0:T(8,128)(2,1)S(1)} %bitcast.5), kind=kOutput, calls=%fused_computation | convolution fusion | flops 4299161600 | bytes 13631488 | tf_op jit(solution)/shard_map/dot_general | solution.py:17
  121.7 0.0 reduce-scatter.3.cloned.1.call-update
  121.7 0.0 reduce-scatter.5.cloned.1.call-start
  121.7 32.8 %all-gather.2.cloned.1.call-done = bf16[1024,4096]{1,0:T(8,128)(2,1)} async-done(((bf16[128,4096]{1,0:T(8,128)(2,1)}), bf16[1024,4096]{1,0:T(8,128)(2,1)}) %all-gather.2.cloned.1.call-update) | async-done | bytes 8388624 | tf_op jit(solution)/shard_map/all_gather | solution.py:23
  154.6 8.4 %convolution_convert_fusion.1 = bf16[4096,512]{1,0:T(8,128)(2,1)S(1)} fusion(bf16[1024,4096]{1,0:T(8,128)(2,1)} %all-gather.2.cloned.1.call-done, bf16[1024,512]{1,0:T(8,128)(2,1)S(1)} %copy-done), kind=kOutput, calls=%fused_computation.1 | convolution fusion | flops 4297064448 | bytes 13631488 | tf_op jit(solution)/shard_map/dot_general | solution.py:26
  163.0 4.4 %convert_element_type.15 = f32[4096,512]{1,0:T(8,128)} convert(bf16[4096,512]{1,0:T(8,128)(2,1)S(1)} %convolution_convert_fusion.1) | non-fusion elementwise | flops 2097152 | bytes 12582912 | tf_op jit(solution)/shard_map/convert_element_type | solution.py:8
  167.4 0.0 reduce-scatter.5.cloned.1.call-update
  167.4 108.3 %reduce-scatter.3.cloned.1.call-done = bf16[128,4096]{1,0:T(8,128)(2,1)} async-done(((bf16[1024,4096]{1,0:T(8,128)(2,1)}), bf16[128,4096]{1,0:T(8,128)(2,1)}) %reduce-scatter.3.cloned.1.call-update) | async-done | bytes 1048592 | tf_op jit(solution)/shard_map/reduce_scatter | solution.py:20
  275.8 2.8 convert_element_type.13
  278.5 128.1 %reduce-scatter.5.cloned.1.call-done = f32[128,512]{1,0:T(8,128)} async-done(((f32[4096,512]{1,0:T(8,128)}), f32[128,512]{1,0:T(8,128)}) %reduce-scatter.5.cloned.1.call-update) | async-done | bytes 262160 | tf_op jit(solution)/shard_map/reduce_scatter | solution.py:30
  406.6 1.7 broadcast_multiply_fusion
Async XLA Ops:
  7.2 107.6 %copy-start = (bf16[1024,512]{1,0:T(8,128)(2,1)S(1)}, bf16[1024,512]{1,0:T(8,128)(2,1)}, u32[]{:S(2)}) copy-start(bf16[1024,512]{1,0:T(8,128)(2,1)} %param.4) | copy-start | bytes 3145732
  7.2 147.4 %all-gather.2.cloned.1.call-start = ((), (), s32[]{:S(2)}) async-start(), calls=%async_computation.4 | async-start | bytes 9437184 | tf_op jit(solution)/shard_map/all_gather | solution.py:23
  7.9 267.9 %reduce-scatter.3.cloned.1.call-start = ((), (), s32[]{:S(2)}) async-start(), calls=%async_computation.3 | async-start | bytes 9437184 | tf_op jit(solution)/shard_map/reduce_scatter | solution.py:20
  121.7 284.9 %reduce-scatter.5.cloned.1.call-start = ((), (), s32[]{:S(2)}) async-start(), calls=%async_computation.5 | async-start | bytes 8650752 | tf_op jit(solution)/shard_map/reduce_scatter | solution.py:30
Sparse Core Ops, SparseCore 0:
  10.6 143.9 all-gather.1
  158.8 116.9 reduce-scatter.2
  278.3 128.2 reduce-scatter.4
